TPU v7x, 32 devices: a whole 2x2x4 slice. The times are simulated.
32 devices in a mesh: dp: 2 (over x), ctx: 4 (over z), tensor: 4 (over y, core).
Axes of the slice: x: 2, y: 2, z: 4, core: 2. Of those that a mesh axis runs over, the one named last changes fastest.
Arguments:
- query_rows: bfloat16 [2, 1024, 5120], P('dp', 'ctx', 'tensor'), may hold values from -6 to 6
- key_rows: bfloat16 [2, 1024, 5120], P('dp', 'ctx', 'tensor'), may hold values from -6 to 6
- value_rows: bfloat16 [2, 1024, 5120], P('dp', 'ctx', 'tensor'), may hold values from -6 to 6
- decay_exp: int32 [40], P('tensor'), may hold values from 1 to 32768, as said below
- out_grad: bfloat16 [2, 1024, 5120], P('dp', 'ctx', 'tensor'), may hold values from -6 to 6
- gain_weight: bfloat16 [40, 128], P('tensor'), may hold values from 0.5 to 1.5
- master_gain: float32 [40, 128], P('tensor', ('dp', 'ctx')), may hold values from 0.5 to 1.5
- first_moment: float32 [40, 128], P('tensor', ('dp', 'ctx')), may hold values from -3 to 3
- second_moment: float32 [40, 128], P('tensor', ('dp', 'ctx')), may hold values from 0.25 to 4
Outputs:
- attn_out: bfloat16 [2, 1024, 5120], P('dp', 'ctx', 'tensor')
- query_grad: bfloat16 [2, 1024, 5120], P('dp', 'ctx', 'tensor')
- key_grad: bfloat16 [2, 1024, 5120], P('dp', 'ctx', 'tensor')
- value_grad: bfloat16 [2, 1024, 5120], P('dp', 'ctx', 'tensor')
- master_new: float32 [40, 128], P('tensor', ('dp', 'ctx'))
- moment_new: float32 [40, 128], P('tensor', ('dp', 'ctx'))
- second_new: float32 [40, 128], P('tensor', ('dp', 'ctx'))
Inputs may be any that keep to these rules, and one draw needn't show every extreme that they name: `decay_exp`: each exponent is a power of two, 2^k with k in 0 to 3 or in 8 to 15.
All inputs are finite; a program needn't handle non-finite values.
Results may differ from a plain program's by a relative error of at most 0.0064.
Values sent between devices are 32-bit elements; how exact they have to be, the bound alone decides.
A program may use at most 64 MiB of HBM per device.

v0:
```python
import math

import jax
import jax.numpy as jnp
from jax import lax
from jax.sharding import PartitionSpec as P

BLOCK = 256
HEAD_DIM = 128


beta_one = 0.9
beta_two = 0.95
learn_rate = 0.02
adam_eps = 1e-08
bias_one = 0.9999734386011124
bias_two = 0.9940794707796667
norm_eps = 1e-05


def entering(x, axis, combine, identity, reverse):
    peers, mine = (lax.axis_size(axis), lax.axis_index(axis))
    everything = jax.tree.map(lambda part: lax.all_gather(part, axis), x)
    start = jax.tree.map(
        lambda part, zero: jnp.broadcast_to(jnp.asarray(zero, part.dtype), part.shape), x, identity
    )

    def hop(k, before):
        at = peers - 1 - k if reverse else k
        reached = at > mine if reverse else at < mine
        new = combine(before, jax.tree.map(lambda part: part[at], everything))
        return jax.tree.map(lambda a, b: jnp.where(reached, a, b), new, before)

    return lax.fori_loop(0, peers, hop, start)


def rounded(value):
    return value.astype(jnp.bfloat16)


def decay_tables(decay_rate):
    position = jnp.arange(BLOCK, dtype=jnp.float32)
    gap_len = position[:, None] - position[None, :]
    decay_mask = jnp.where(
        gap_len >= 0, jnp.exp(-decay_rate[:, None, None] * jnp.maximum(gap_len, 0.0)), 0.0
    )
    query_decay = jnp.exp(-decay_rate[:, None] * position[None, :])
    key_decay = jnp.exp(-decay_rate[:, None] * (BLOCK - position)[None, :])
    block_decay = jnp.exp(-decay_rate * BLOCK)
    return (decay_mask, query_decay, key_decay, block_decay)


def combine_states(earlier, later):
    return (later[1][None, :, None, None] * earlier[0] + later[0], earlier[1] * later[1])


def piece_of(rows, head, blk_index):
    return rows[
        :, blk_index * BLOCK : (blk_index + 1) * BLOCK, head * HEAD_DIM : (head + 1) * HEAD_DIM
    ]


def body(
    query_rows,
    key_rows,
    value_rows,
    decay_exp,
    out_grad,
    gain_weight,
    master_gain,
    first_moment,
    second_moment,
):
    batch_dev, local_len, row_width = query_rows.shape
    heads_dev = row_width // HEAD_DIM
    n_blocks = local_len // BLOCK
    seq_len = local_len * lax.axis_size("ctx")
    token_count = batch_dev * lax.axis_size("dp") * seq_len
    channels = row_width * lax.axis_size("tensor")
    decay_rate = decay_exp.astype(jnp.float32) * (math.log(2.0) / (4.0 * seq_len))
    decay_mask, query_decay, key_decay, block_decay = decay_tables(decay_rate)
    weight_store = {}
    intra_store = {}
    summary_store = {}
    local_list = []
    for head in range(heads_dev):
        key_col = key_decay[head][:, None]
        head_state = jnp.zeros((batch_dev, HEAD_DIM, HEAD_DIM), jnp.float32)
        blk_index = 0
        query_blk = piece_of(query_rows, head, blk_index)
        key_blk = piece_of(key_rows, head, blk_index)
        value_blk = piece_of(value_rows, head, blk_index)
        scores = jnp.einsum("btd,bsd->bts", query_blk, key_blk, preferred_element_type=jnp.float32)
        weights = rounded(scores * decay_mask[head][None])
        weight_store[head, blk_index] = weights
        intra_store[head, blk_index] = jnp.einsum(
            "bts,bsd->btd", weights, value_blk, preferred_element_type=jnp.float32
        )
        key_scaled = rounded(key_col * key_blk)
        summary = jnp.einsum(
            "bsd,bse->bde", key_scaled, value_blk, preferred_element_type=jnp.float32
        )
        summary_store[head, blk_index] = summary
        head_state = block_decay[head] * head_state + summary
        local_list.append(head_state)
    local_state = jnp.stack(local_list, axis=1)
    device_decay = jnp.exp(-decay_rate * local_len)
    identity = (jnp.zeros_like(local_state), jnp.ones_like(device_decay))
    run_state = entering((local_state, device_decay), "ctx", combine_states, identity, False)[0]
    low_store = {}
    head_cols = []
    for head in range(heads_dev):
        query_col = query_decay[head][:, None]
        head_state = run_state[:, head]
        blk_index = 0
        state_low = rounded(head_state)
        low_store[head, blk_index] = state_low
        inter_term = jnp.einsum(
            "btd,bde->bte",
            piece_of(query_rows, head, blk_index),
            state_low,
            preferred_element_type=jnp.float32,
        )
        block_rows = intra_store[head, blk_index] + query_col * inter_term
        head_state = block_decay[head] * head_state + summary_store[head, blk_index]
        head_cols.append(block_rows)
    attn_all = jnp.concatenate(head_cols, axis=2)
    gain_full = gain_weight.reshape(-1).astype(jnp.float32)
    square_sum = lax.psum(jnp.sum(attn_all * attn_all, axis=2), "tensor")
    inv_rms = lax.rsqrt(square_sum / channels + norm_eps)[:, :, None]
    attn_out = rounded(gain_full * attn_all * inv_rms)
    grad_full = out_grad.astype(jnp.float32)
    scaled_grad = grad_full * gain_full
    dot_sum = lax.psum(jnp.sum(scaled_grad * attn_all, axis=2), "tensor")
    mean_dot = (dot_sum / channels)[:, :, None]
    grad_low = rounded(inv_rms * (scaled_grad - attn_all * inv_rms * inv_rms * mean_dot))
    gain_term = jnp.sum(grad_full * attn_all * inv_rms, axis=(0, 1)).reshape(heads_dev, HEAD_DIM)
    back_store = {}
    upward_list = []
    for head in range(heads_dev):
        query_col = query_decay[head][:, None]
        upward = jnp.zeros((batch_dev, HEAD_DIM, HEAD_DIM), jnp.float32)
        for blk_index in reversed(range(n_blocks)):
            query_scaled = rounded(query_col * piece_of(query_rows, head, blk_index))
            part_sum = jnp.einsum(
                "btd,bte->bde",
                query_scaled,
                piece_of(grad_low, head, blk_index),
                preferred_element_type=jnp.float32,
            )
            back_store[head, blk_index] = part_sum
            upward = block_decay[head] * upward + part_sum
        upward_list.append(upward)
    upward_all = jnp.stack(upward_list, axis=1)
    back_carry = entering((upward_all, device_decay), "ctx", combine_states, identity, True)[0]
    query_cols = []
    key_cols = []
    value_cols = []
    for head in range(heads_dev):
        query_col = query_decay[head][:, None]
        key_col = key_decay[head][:, None]
        carry_head = back_carry[:, head]
        query_blocks = [None] * n_blocks
        key_blocks = [None] * n_blocks
        value_blocks = [None] * n_blocks
        for blk_index in reversed(range(n_blocks)):
            query_blk = piece_of(query_rows, head, blk_index)
            key_blk = piece_of(key_rows, head, blk_index)
            value_blk = piece_of(value_rows, head, blk_index)
            grad_blk = piece_of(grad_low, head, blk_index)
            back_low = rounded(carry_head)
            dweights = rounded(
                jnp.einsum("bte,bse->bts", grad_blk, value_blk, preferred_element_type=jnp.float32)
                * decay_mask[head][None]
            )
            query_part = jnp.einsum(
                "bts,bsd->btd", dweights, key_blk, preferred_element_type=jnp.float32
            )
            query_part = query_part + query_col * jnp.einsum(
                "bte,bde->btd",
                grad_blk,
                low_store[head, blk_index],
                preferred_element_type=jnp.float32,
            )
            key_part = jnp.einsum(
                "bts,btd->bsd", dweights, query_blk, preferred_element_type=jnp.float32
            )
            key_part = key_part + key_col * jnp.einsum(
                "bse,bde->bsd", value_blk, back_low, preferred_element_type=jnp.float32
            )
            value_part = jnp.einsum(
                "bts,bte->bse",
                weight_store[head, blk_index],
                grad_blk,
                preferred_element_type=jnp.float32,
            )
            value_part = value_part + key_col * jnp.einsum(
                "bsd,bde->bse", key_blk, back_low, preferred_element_type=jnp.float32
            )
            query_blocks[blk_index] = rounded(query_part)
            key_blocks[blk_index] = rounded(key_part)
            value_blocks[blk_index] = rounded(value_part)
            carry_head = block_decay[head] * carry_head + back_store[head, blk_index]
        query_cols.append(query_blocks[0])
        key_cols.append(key_blocks[0])
        value_cols.append(value_blocks[0])
    query_grad = jnp.concatenate(query_cols, axis=2)
    key_grad = jnp.concatenate(key_cols, axis=2)
    value_grad = jnp.concatenate(value_cols, axis=2)
    partial_sum = lax.psum_scatter(gain_term, "dp", scatter_dimension=1, tiled=True)
    grad_share = lax.psum_scatter(partial_sum, "ctx", scatter_dimension=1, tiled=True)
    gain_grad = grad_share / math.sqrt(token_count)
    moment_new = beta_one * first_moment + (1.0 - beta_one) * gain_grad
    second_new = beta_two * second_moment + (1.0 - beta_two) * gain_grad * gain_grad
    master_new = master_gain - learn_rate * (moment_new / bias_one) / (
        jnp.sqrt(second_new / bias_two) + adam_eps
    )
    return (attn_out, query_grad, key_grad, value_grad, master_new, moment_new, second_new)


def solution(mesh):
    return jax.shard_map(
        body,
        mesh=mesh,
        in_specs=(
            P("dp", "ctx", "tensor"),
            P("dp", "ctx", "tensor"),
            P("dp", "ctx", "tensor"),
            P("tensor"),
            P("dp", "ctx", "tensor"),
            P("tensor", None),
            P("tensor", ("dp", "ctx")),
            P("tensor", ("dp", "ctx")),
            P("tensor", ("dp", "ctx")),
        ),
        out_specs=(
            P("dp", "ctx", "tensor"),
            P("dp", "ctx", "tensor"),
            P("dp", "ctx", "tensor"),
            P("dp", "ctx", "tensor"),
            P("tensor", ("dp", "ctx")),
            P("tensor", ("dp", "ctx")),
            P("tensor", ("dp", "ctx")),
        ),
        check_vma=False,
    )
```

profile of v0, /device:TPU:0, one launch (start us, length us, event | category | flops | bytes accessed | tf_op | source)
XLA Modules:
  0.0 263.3 jit_solution(4358091460561496750)
XLA Ops:
  7.3 1.3 dynamic-slice
  20.2 1.2 fusion.244
  21.4 1.2 fusion.242
  27.3 13.6 %all-reduce = f32[40]{0:T(128)S(1)} all-reduce(f32[40]{0:T(128)S(1)} %get-tuple-element.363), channel_id=2, replica_groups=mesh['dp'=2,'ctx'=4,'tensor'=4] {'ctx'}, use_global_device_ids=true, to_apply=%add | all-reduce | flops 40 | bytes 320
  50.7 32.9 %all-gather.6.cloned.1.call-done = f32[4,10,128,128]{3,2,1,0:T(8,128)} async-done(((f32[1,10,128,128]{3,2,1,0:T(8,128)}), f32[4,10,128,128]{3,2,1,0:T(8,128)}) %all-gather.6.cloned.1.call-update) | async-done | bytes 2621456 | tf_op jit(solution)/shard_map/all_gather | solution.py:23
  83.7 11.5 %while.30 = (s32[]{:T(128)}, f32[1,10,128,128]{3,2,1,0:T(8,128)}, s32[]{:T(128)}, f32[4,10]{1,0:T(4,128)}, f32[4,1,10,128,128]{4,3,2,1,0:T(8,128)}, /*index=5*/s32[]{:T(128)}, s32[]{:T(128)}) while((s32[]{:T(128)}, f32[1,10,128,128]{3,2,1,0:T(8,128)}, s32[]{:T(128)}, f32[4,10]{1,0:T(4,128)}, f32[4,1,10,128,128]{4,3,2,1,0:T(8,128)}, ...), condition=%wide.region_1.2_spmd.clone, body=%wide.region_0.1_spmd.clone.sunk | while | flops 655364 | bytes 1966313 | solution.py:34
  84.3 2.1 fusion.577
  87.1 2.3 fusion.577
  90.0 2.3 fusion.577
  92.9 2.3 fusion.577
  95.3 1.2 convert.25
  96.5 1.2 fusion.118
  104.1 6.4 %psum.14 = f32[1,256]{1,0:T(1,128)S(1)} all-reduce(f32[1,256]{1,0:T(1,128)S(1)} %bitcast.1109), channel_id=1, replica_groups=mesh['dp'=2,'ctx'=4,'tensor'=4] {'tensor'}, use_global_device_ids=true, to_apply=%region_3.4 | all-reduce | flops 256 | bytes 2048 | tf_op jit(solution)/shard_map/psum | solution.py:129
  111.1 2.6 fusion.8
  113.8 6.5 %psum.15 = f32[1,256]{1,0:T(1,128)} all-reduce(f32[1,256]{1,0:T(1,128)} %bitcast.1108), channel_id=1, replica_groups=mesh['dp'=2,'ctx'=4,'tensor'=4] {'tensor'}, use_global_device_ids=true, to_apply=%region_5.6 | all-reduce | flops 256 | bytes 2048 | tf_op jit(solution)/shard_map/psum | solution.py:134
  120.9 2.8 %fusion.6 = (bf16[1,256,1280]{1,2,0:T(8,128)(2,1)S(1)}, bf16[1,256,1280]{1,2,0:T(8,128)(2,1)}) fusion(bf16[1,256,1280]{1,2,0:T(8,128)(2,1)} %copy.24, f32[1,256,1280]{1,2,0:T(8,128)} %copy-done, f32[256]{0:T(256)S(1)} %bitcast.1107, f32[256]{0:T(256)} %bitcast.1105, f32[1280]{0:T(1024)S(1)} %bitcast_convert_fusion), kind=kLoop, calls=%fused_computation.13 | loop fusion | flops 3604480 | bytes 3283968 | tf_op jit(solution)/shard_map/convert_element_type | solution.py:38
  123.8 1.6 convolution_multiply_fusion.9
  126.3 1.6 convolution_multiply_fusion.8
  128.7 1.6 convolution_multiply_fusion.7
  131.1 1.6 convolution_multiply_fusion.6
  146.8 1.7 fusion.67
  148.5 6.6 %reduce-scatter.7.cloned.1.call-done = f32[64,10]{1,0:T(8,128)} async-done(((f32[128,10]{1,0:T(8,128)}), f32[64,10]{1,0:T(8,128)}) %reduce-scatter.7.cloned.1.call-update) | async-done | bytes 2576
  155.4 1.7 fusion.68
  157.2 2.2 copy.26
  169.3 2.2 copy.27
  171.5 5.2 %reduce-scatter.9.cloned.1.call-done = f32[16,10]{1,0:T(8,128)} async-done(((f32[64,10]{1,0:T(8,128)}), f32[16,10]{1,0:T(8,128)}) %reduce-scatter.9.cloned.1.call-update) | async-done | bytes 656
  178.1 52.9 %all-gather.8.cloned.1.call-done = f32[4,10,128,128]{3,2,1,0:T(8,128)} async-done(((f32[1,10,128,128]{3,2,1,0:T(8,128)}), f32[4,10,128,128]{3,2,1,0:T(8,128)}) %all-gather.8.cloned.1.call-update) | async-done | bytes 2621456 | tf_op jit(solution)/shard_map/all_gather | solution.py:23
  231.0 7.8 %while.31 = (s32[]{:T(128)}, f32[1,10,128,128]{3,2,1,0:T(8,128)S(1)}, s32[]{:T(128)}, f32[4,10]{1,0:T(4,128)}, f32[4,1,10,128,128]{4,3,2,1,0:T(8,128)}, /*index=5*/s32[]{:T(128)}, s32[]{:T(128)}, s32[]{:T(128)}, s32[]{:T(128)}) while((s32[]{:T(128)}, f32[1,10,128,128]{3,2,1,0:T(8,128)S(1)}, s32[]{:T(128)}, f32[4,10]{1,0:T(4,128)}, ...), condition=%wide.region_7.8_spmd.clone, body=%wide.region_6.7_spmd.clone.sunk | while | flops 655368 | bytes 1966375 | solution.py:34
  231.7 1.2 fusion.578
  233.7 1.2 fusion.578
  235.6 1.2 fusion.578
  237.5 1.2 fusion.578
  (377 shorter events, 77.3 us)
Async XLA Ops:
  7.2 16.5 %copy-start.3 = (bf16[1,256,1280]{2,1,0:T(8,128)(2,1)S(1)}, bf16[1,256,1280]{2,1,0:T(8,128)(2,1)}, u32[]{:S(2)}) copy-start(bf16[1,256,1280]{2,1,0:T(8,128)(2,1)} %param.15) | copy-start | bytes 1966084
  7.2 16.5 %copy-start.11 = (bf16[1,256,1280]{2,1,0:T(8,128)(2,1)S(1)}, bf16[1,256,1280]{2,1,0:T(8,128)(2,1)}, u32[]{:S(2)}) copy-start(bf16[1,256,1280]{2,1,0:T(8,128)(2,1)} %param.14) | copy-start | bytes 1966084
  7.2 76.5 %all-gather.6.cloned.1.call-start = ((), (), s32[]{:S(2)}) async-start(), calls=%async_computation.2 | async-start | bytes 3276800 | tf_op jit(solution)/shard_map/all_gather | solution.py:23
  10.7 15.3 %copy-start.66 = (f32[1,256]{1,0:T(1,128)}, f32[1,256]{1,0:T(1,128)S(1)}, u32[]{:S(2)}) copy-start(f32[1,256]{1,0:T(1,128)S(1)} %get-tuple-element.342) | copy-start | bytes 3076
  10.7 15.3 %copy-start.68 = (f32[1,256]{1,0:T(1,128)}, f32[1,256]{1,0:T(1,128)S(1)}, u32[]{:S(2)}) copy-start(f32[1,256]{1,0:T(1,128)S(1)} %get-tuple-element.343) | copy-start | bytes 3076
  10.7 15.3 %copy-start.70 = (f32[1,256]{1,0:T(1,128)}, f32[1,256]{1,0:T(1,128)S(1)}, u32[]{:S(2)}) copy-start(f32[1,256]{1,0:T(1,128)S(1)} %get-tuple-element.344) | copy-start | bytes 3076
  10.7 15.3 %copy-start.72 = (f32[1,256]{1,0:T(1,128)}, f32[1,256]{1,0:T(1,128)S(1)}, u32[]{:S(2)}) copy-start(f32[1,256]{1,0:T(1,128)S(1)} %get-tuple-element.345) | copy-start | bytes 3076
  10.7 15.3 %copy-start.74 = (f32[1,256]{1,0:T(1,128)}, f32[1,256]{1,0:T(1,128)S(1)}, u32[]{:S(2)}) copy-start(f32[1,256]{1,0:T(1,128)S(1)} %get-tuple-element.346) | copy-start | bytes 3076
  10.7 15.3 %copy-start.76 = (f32[1,256]{1,0:T(1,128)}, f32[1,256]{1,0:T(1,128)S(1)}, u32[]{:S(2)}) copy-start(f32[1,256]{1,0:T(1,128)S(1)} %get-tuple-element.347) | copy-start | bytes 3076
  10.8 15.3 %copy-start.78 = (f32[1,256]{1,0:T(1,128)}, f32[1,256]{1,0:T(1,128)S(1)}, u32[]{:S(2)}) copy-start(f32[1,256]{1,0:T(1,128)S(1)} %get-tuple-element.348) | copy-start | bytes 3076
  10.8 15.3 %copy-start.80 = (f32[1,256]{1,0:T(1,128)}, f32[1,256]{1,0:T(1,128)S(1)}, u32[]{:S(2)}) copy-start(f32[1,256]{1,0:T(1,128)S(1)} %get-tuple-element.349) | copy-start | bytes 3076
  10.8 15.3 %copy-start.82 = (f32[1,256]{1,0:T(1,128)}, f32[1,256]{1,0:T(1,128)S(1)}, u32[]{:S(2)}) copy-start(f32[1,256]{1,0:T(1,128)S(1)} %get-tuple-element.350) | copy-start | bytes 3076
  10.8 15.3 %copy-start.84 = (f32[1,256]{1,0:T(1,128)}, f32[1,256]{1,0:T(1,128)S(1)}, u32[]{:S(2)}) copy-start(f32[1,256]{1,0:T(1,128)S(1)} %get-tuple-element.351) | copy-start | bytes 3076
  26.1 129.0 %reduce-scatter.7.cloned.1.call-start = ((), (), s32[]{:S(2)}) async-start(), calls=%async_computation.4 | async-start | bytes 98304
  50.7 49.5 %copy-start.86 = (f32[1,256]{1,0:T(1,128)}, f32[1,256]{1,0:T(1,128)S(1)}, u32[]{:S(2)}) copy-start(f32[1,256]{1,0:T(1,128)S(1)} %get-tuple-element.332) | copy-start | bytes 3076
  123.8 21.3 %copy-start.1 = (bf16[1,256,1280]{1,2,0:T(8,128)(2,1)}, bf16[1,256,1280]{1,2,0:T(8,128)(2,1)S(1)}, u32[]{:S(2)}) copy-start(bf16[1,256,1280]{1,2,0:T(8,128)(2,1)S(1)} %get-tuple-element.330) | copy-start | bytes 1966084
  123.8 7.3 %copy-start.103 = (f32[1,256]{1,0:T(1,128)S(1)}, f32[1,256]{1,0:T(1,128)}, u32[]{:S(2)}) copy-start(f32[1,256]{1,0:T(1,128)} %get-tuple-element.338) | copy-start | bytes 3076
  135.2 8.0 %copy-start.91 = (f32[1,256]{1,0:T(1,128)S(1)}, f32[1,256]{1,0:T(1,128)}, u32[]{:S(2)}) copy-start(f32[1,256]{1,0:T(1,128)} %get-tuple-element.334) | copy-start | bytes 3076
  136.1 8.1 %copy-start.89 = (f32[1,256]{1,0:T(1,128)S(1)}, f32[1,256]{1,0:T(1,128)}, u32[]{:S(2)}) copy-start(f32[1,256]{1,0:T(1,128)} %get-tuple-element.333) | copy-start | bytes 3076
  136.1 9.0 %copy-start.87 = (f32[1,256]{1,0:T(1,128)S(1)}, f32[1,256]{1,0:T(1,128)}, u32[]{:S(2)}) copy-start(f32[1,256]{1,0:T(1,128)} %copy-done.86) | copy-start | bytes 3076
  146.7 30.0 %reduce-scatter.9.cloned.1.call-start = ((), (), s32[]{:S(2)}) async-start(), calls=%async_computation.5 | async-start | bytes 40960
  148.5 10.9 %copy-start.101 = (f32[1,256]{1,0:T(1,128)S(1)}, f32[1,256]{1,0:T(1,128)}, u32[]{:S(2)}) copy-start(f32[1,256]{1,0:T(1,128)} %get-tuple-element.337) | copy-start | bytes 3076
  155.2 75.8 %all-gather.8.cloned.1.call-start = ((), (), s32[]{:S(2)}) async-start(), calls=%async_computation.3 | async-start | bytes 3276800 | tf_op jit(solution)/shard_map/all_gather | solution.py:23
  166.7 10.7 %copy-start.109 = (f32[10,16]{1,0:T(8,128)S(1)}, f32[10,16]{1,0:T(8,128)}, u32[]{:S(2)}) copy-start(f32[10,16]{1,0:T(8,128)} %param.19) | copy-start | bytes 1924
  166.7 10.7 %copy-start.110 = (f32[10,16]{1,0:T(8,128)S(1)}, f32[10,16]{1,0:T(8,128)}, u32[]{:S(2)}) copy-start(f32[10,16]{1,0:T(8,128)} %param.20) | copy-start | bytes 1924
  166.7 10.7 %copy-start.111 = (f32[10,16]{1,0:T(8,128)S(1)}, f32[10,16]{1,0:T(8,128)}, u32[]{:S(2)}) copy-start(f32[10,16]{1,0:T(8,128)} %param.21) | copy-start | bytes 1924
  231.0 7.9 %copy-start.6 = (bf16[1,256,1280]{2,1,0:T(8,128)(2,1)S(1)}, bf16[1,256,1280]{2,1,0:T(8,128)(2,1)}, u32[]{:S(2)}) copy-start(bf16[1,256,1280]{2,1,0:T(8,128)(2,1)} %param.15) | copy-start | bytes 1966084
  231.0 7.9 %copy-start.85 = (f32[1,256]{1,0:T(1,128)S(1)}, f32[1,256]{1,0:T(1,128)}, u32[]{:S(2)}) copy-start(f32[1,256]{1,0:T(1,128)} %copy-done.84) | copy-start | bytes 3076
  231.0 8.1 %copy-start.83 = (f32[1,256]{1,0:T(1,128)S(1)}, f32[1,256]{1,0:T(1,128)}, u32[]{:S(2)}) copy-start(f32[1,256]{1,0:T(1,128)} %copy-done.82) | copy-start | bytes 3076
  240.7 8.7 %copy-start.10 = (bf16[1,256,1280]{2,1,0:T(8,128)(2,1)S(1)}, bf16[1,256,1280]{2,1,0:T(8,128)(2,1)}, u32[]{:S(2)}) copy-start(bf16[1,256,1280]{2,1,0:T(8,128)(2,1)} %param.13) | copy-start | bytes 1966084
  240.7 8.7 %copy-start.45 = (bf16[256,256]{1,0:T(8,128)(2,1)S(1)}, bf16[256,256]{1,0:T(8,128)(2,1)}, u32[]{:S(2)}) copy-start(bf16[256,256]{1,0:T(8,128)(2,1)} %fusion.59) | copy-start | bytes 393220
  240.9 8.7 %copy-start.43 = (bf16[256,256]{1,0:T(8,128)(2,1)S(1)}, bf16[256,256]{1,0:T(8,128)(2,1)}, u32[]{:S(2)}) copy-start(bf16[256,256]{1,0:T(8,128)(2,1)} %fusion.60) | copy-start | bytes 393220
  (85 other events, 261.0 us)
Sparse Core Ops, SparseCore 0:
  26.1 57.4 all-gather.5
  146.9 8.2 reduce-scatter.6
  157.4 19.2 reduce-scatter.8
  178.1 52.8 all-gather.7
where the time goes:
time: 265 us; the launch traced here: 263 us
  waiting for transfers between devices  97.7 us (37%)
  matrix products  70.3 us (27%)
  blocking collectives  26.5 us (10%)
  other arithmetic  24 us (9%)
  between operations  22.4 us (8%)
  local copies, waits for them, and re-layouts  22.1 us (8%)
    all_gather x2, waiting for transfers between devices, entering(): everything = jax.tree.map(lambda part: lax.all_gather(part, axis), x)  85.8 us
    unnamed x235, local copies, waits for them, and re-layouts  14.7 us
    select_n x8, other arithmetic, hop(): return jax.tree.map(lambda a, b: jnp.where(reached, a, b), new, before)  13.8 us
    unnamed x1, blocking collectives  13.6 us
    unnamed x6, waiting for transfers between devices  11.9 us
    dot_general x10, matrix products, body(): jnp.einsum('bte,bse->bts', grad_blk, value_blk, preferred_element_type=jn...  10.3 us
    dot_general x10, matrix products, body(): jnp.einsum('btd,bte->bde', query_scaled, piece_of(grad_low, head, blk_ind...  9.01 us
    dot_general x10, matrix products, body(): jnp.einsum('bts,bsd->btd', dweights, key_blk, preferred_element_type=jnp....  8.51 us
  transfers between devices with their start and end apart: 4, of which 4 were waited for; matrix products, arithmetic and copies ran while one was open for 11% of the time, Pallas kernels for 0%

commit v1 on v0

v1 whole, which is shorter than its diff:
```python
import functools
import math

import jax
import jax.numpy as jnp
from jax import lax
from jax.experimental import pallas as pl
from jax.experimental.pallas import tpu as pltpu
from jax.sharding import PartitionSpec as P

HEAD_DIM = 128
MESH = pl.DeviceIdType.MESH

beta_one = 0.9
beta_two = 0.95
learn_rate = 0.02
adam_eps = 1e-08
bias_one = 0.9999734386011124
bias_two = 0.9940794707796667
norm_eps = 1e-05

LOW = jnp.bfloat16
F32 = jnp.float32


def dot(a, b, dim_a, dim_b, precision=None):
    return lax.dot_general(
        a, b, (((dim_a,), (dim_b,)), ((), ())), preferred_element_type=F32, precision=precision
    )


def fused(
    dims,
    exp_ref,
    query_hbm,
    key_hbm,
    value_hbm,
    grad_hbm,
    gain_ref,
    master_ref,
    first_ref,
    second_ref,
    attn_hbm,
    qgrad_hbm,
    kgrad_hbm,
    vgrad_hbm,
    master_out,
    moment_out,
    second_out,
    query_v,
    key_v,
    value_v,
    grad_v,
    attn_v,
    mask_v,
    weight_v,
    low_v,
    local_v,
    fwd_in,
    fwd_out,
    bwd_in,
    bwd_out,
    gl_v,
    ao_v,
    qg_v,
    kg_v,
    vg_v,
    gain_v,
    gpart_v,
    square_acc,
    dot_acc,
    norm_mine,
    norm_in,
    ctx_in,
    dp_mine,
    dp_in,
    in_sem,
    out_sem,
    fs_sem,
    fr_sem,
    bs_sem,
    br_sem,
    ts_sem,
    tr_sem,
    cs_sem,
    cr_sem,
    ds_sem,
    dr_sem,
):
    heads, length, n_dp, n_ctx, n_tensor = dims
    seq_len = length * n_ctx
    channels = heads * HEAD_DIM * n_tensor
    token_count = n_dp * seq_len
    at_dp, at_ctx, at_tensor = (lax.axis_index(name) for name in ("dp", "ctx", "tensor"))
    later = lax.rem(at_ctx + 1, n_ctx)
    earlier = lax.rem(at_ctx + n_ctx - 1, n_ctx)
    is_first, is_last = at_ctx == 0, at_ctx == n_ctx - 1

    def columns(h):
        return pl.ds(pl.multiple_of(h * HEAD_DIM, HEAD_DIM), HEAD_DIM)

    pairs = ((key_hbm, key_v), (value_hbm, value_v), (query_hbm, query_v), (grad_hbm, grad_v))

    def load(which, h):
        hbm, vmem = pairs[which]
        return pltpu.make_async_copy(hbm.at[:, columns(h)], vmem.at[h], in_sem.at[which, h])

    outs = ((ao_v, attn_hbm), (qg_v, qgrad_hbm), (kg_v, kgrad_hbm), (vg_v, vgrad_hbm))

    def save(which, h):
        vmem, hbm = outs[which]
        return pltpu.make_async_copy(vmem.at[h], hbm.at[:, columns(h)], out_sem.at[which, h])

    def loop(low, high, step):
        lax.fori_loop(low, high, lambda h, c: (step(h), c)[1], 0)

    def start_kv(h):
        load(0, h).start()
        load(1, h).start()

    def start_qg(h):
        load(2, h).start()
        load(3, h).start()

    loop(0, heads, start_kv)
    loop(0, heads, start_qg)

    barrier = pltpu.get_barrier_semaphore()
    groups = (("dp", at_dp, n_dp), ("ctx", at_ctx, n_ctx), ("tensor", at_tensor, n_tensor))
    for name, mine, count in groups:
        for d in range(1, count):
            pl.semaphore_signal(
                barrier, inc=1, device_id={name: lax.rem(mine + d, count)}, device_id_type=MESH
            )
    pl.semaphore_wait(barrier, n_dp + n_ctx + n_tensor - 3)

    def share(name, mine, count, source, slots, send_sem, recv_sem):
        return [
            pltpu.make_async_remote_copy(
                src_ref=source,
                dst_ref=slots.at[d - 1],
                send_sem=send_sem.at[d - 1],
                recv_sem=recv_sem.at[d - 1],
                device_id={name: lax.rem(mine + d, count)},
                device_id_type=MESH,
            )
            for d in range(1, count)
        ]

    def forward_copy(h):
        return pltpu.make_async_remote_copy(
            src_ref=fwd_out.at[h],
            dst_ref=fwd_in.at[h],
            send_sem=fs_sem.at[h],
            recv_sem=fr_sem.at[h],
            device_id={"ctx": later},
            device_id_type=MESH,
        )

    def backward_copy(h):
        return pltpu.make_async_remote_copy(
            src_ref=bwd_out.at[h],
            dst_ref=bwd_in.at[h],
            send_sem=bs_sem.at[h],
            recv_sem=br_sem.at[h],
            device_id={"ctx": earlier},
            device_id_type=MESH,
        )

    gain_v[...] = gain_ref[...].astype(F32)
    row = lax.broadcasted_iota(jnp.int32, (length, HEAD_DIM), 0).astype(F32)

    def rate_of(h):
        return exp_ref[h].astype(F32) * (math.log(2.0) / (4.0 * seq_len))

    def key_decay(h):
        return jnp.exp(-rate_of(h) * (length - row))

    def query_decay(h):
        return jnp.exp(-rate_of(h) * row)

    def block_decay(h):
        return jnp.exp(jnp.full((HEAD_DIM, HEAD_DIM), -rate_of(h) * length, F32))

    def summarize(h):
        load(0, h).wait()
        load(1, h).wait()
        scaled = (key_decay(h) * key_v[h].astype(F32)).astype(LOW)
        summary = dot(scaled, value_v[h], 0, 0)

        @pl.when(is_first)
        def _():
            fwd_out[h] = summary
            forward_copy(h).start()

        @pl.when(jnp.logical_not(is_first))
        def _():
            local_v[h] = summary

    loop(0, heads, summarize)
    square_acc[...] = jnp.zeros_like(square_acc)
    dot_acc[...] = jnp.zeros_like(dot_acc)

    def attend(h):
        load(2, h).wait()
        load(3, h).wait()
        gap = (
            lax.broadcasted_iota(jnp.int32, (length, length), 0)
            - lax.broadcasted_iota(jnp.int32, (length, length), 1)
        ).astype(F32)
        mask = jnp.where(gap >= 0, jnp.exp(-rate_of(h) * jnp.maximum(gap, 0.0)), 0.0)
        mask_v[h] = mask
        query = query_v[h]
        weights = (dot(query, key_v[h], 1, 1) * mask).astype(LOW)
        weight_v[h] = weights
        attn_v[h] = dot(weights, value_v[h], 1, 0)

        @pl.when(is_first)
        def _():
            low_v[h] = jnp.zeros((HEAD_DIM, HEAD_DIM), LOW)

        @pl.when(jnp.logical_not(is_first))
        def _():
            forward_copy(h).wait_recv()

            @pl.when(jnp.logical_not(is_last))
            def _():
                fwd_out[h] = block_decay(h) * fwd_in[h] + local_v[h]
                forward_copy(h).start()

            low_v[h] = fwd_in[h].astype(LOW)

        attn = attn_v[h] + query_decay(h) * dot(query_v[h], low_v[h], 1, 0)
        attn_v[h] = attn
        square_acc[...] += attn * attn
        dot_acc[...] += grad_v[h].astype(F32) * gain_v[pl.ds(h, 1), :] * attn

    loop(0, heads, attend)

    exact = lax.Precision.HIGHEST
    ones = jnp.ones((8, HEAD_DIM), F32)
    upper = lax.broadcasted_iota(jnp.int32, (8, length), 0) < 4
    norm_mine[...] = jnp.where(
        upper, dot(ones, square_acc[...], 1, 1, exact), dot(ones, dot_acc[...], 1, 1, exact)
    )
    norm_copies = share("tensor", at_tensor, n_tensor, norm_mine, norm_in, ts_sem, tr_sem)
    for copy in norm_copies:
        copy.start()
    total = norm_mine[...]
    for d, copy in enumerate(norm_copies):
        copy.wait_recv()
        total = total + norm_in[d]
    pick = lax.broadcasted_iota(jnp.int32, (8, HEAD_DIM), 0)
    square_sum = dot(total, (pick == 0).astype(F32), 0, 0, exact)
    dot_sum = dot(total, (pick == 4).astype(F32), 0, 0, exact)
    inv_rms = lax.rsqrt(square_sum / channels + norm_eps)
    mean_dot = dot_sum / channels
    square_acc[...] = inv_rms
    dot_acc[...] = inv_rms * inv_rms * mean_dot

    def back_summary(h):
        attn = attn_v[h]
        inverse = square_acc[...]
        gain = gain_v[pl.ds(h, 1), :]
        grad = grad_v[h].astype(F32)
        grad_low = (inverse * (grad * gain - attn * dot_acc[...])).astype(LOW)
        gl_v[h] = grad_low
        scaled = (query_decay(h) * query_v[h].astype(F32)).astype(LOW)
        part = dot(scaled, grad_low, 0, 0)

        @pl.when(is_last)
        def _():
            bwd_out[h] = part
            backward_copy(h).start()

        @pl.when(jnp.logical_not(is_last))
        def _():
            local_v[h] = part

        normed = attn * inverse
        ao_v[h] = (gain * normed).astype(LOW)
        save(0, h).start()
        gpart_v[pl.ds(h, 1), :] = jnp.sum(grad * normed, axis=0, keepdims=True)

    loop(0, heads, back_summary)
    ctx_copies = share("ctx", at_ctx, n_ctx, gpart_v, ctx_in, cs_sem, cr_sem)
    for copy in ctx_copies:
        copy.start()

    def gradients(h):
        grad_low = gl_v[h]
        dweights = (dot(grad_low, value_v[h], 1, 1) * mask_v[h]).astype(LOW)
        query_part = dot(dweights, key_v[h], 1, 0)
        query_part += query_decay(h) * dot(grad_low, low_v[h], 1, 1)
        qg_v[h] = query_part.astype(LOW)
        save(1, h).start()
        key_part = dot(dweights, query_v[h], 0, 0)
        value_part = dot(weight_v[h], grad_low, 0, 0)

        @pl.when(is_last)
        def _():
            kg_v[h] = key_part.astype(LOW)
            vg_v[h] = value_part.astype(LOW)

        @pl.when(jnp.logical_not(is_last))
        def _():
            backward_copy(h).wait_recv()

            @pl.when(jnp.logical_not(is_first))
            def _():
                bwd_out[h] = block_decay(h) * bwd_in[h] + local_v[h]
                backward_copy(h).start()

            back_low = bwd_in[h].astype(LOW)
            decay = key_decay(h)
            kg_v[h] = (key_part + decay * dot(value_v[h], back_low, 1, 1)).astype(LOW)
            vg_v[h] = (value_part + decay * dot(key_v[h], back_low, 1, 0)).astype(LOW)

        save(2, h).start()
        save(3, h).start()

    third = heads // 3
    loop(0, third, gradients)
    gain_sum = gpart_v[...]
    for d, copy in enumerate(ctx_copies):
        copy.wait_recv()
        gain_sum = gain_sum + ctx_in[d]
    dp_mine[...] = gain_sum
    dp_copies = share("dp", at_dp, n_dp, dp_mine, dp_in, ds_sem, dr_sem)
    for copy in dp_copies:
        copy.start()
    loop(third, heads - 1, gradients)

    gain_sum = dp_mine[...]
    for d, copy in enumerate(dp_copies):
        copy.wait_recv()
        gain_sum = gain_sum + dp_in[d]
    width = master_ref.shape[1]
    place = (at_dp * n_ctx + at_ctx) * width
    chosen = lax.broadcasted_iota(jnp.int32, (HEAD_DIM, width), 0) == (
        lax.broadcasted_iota(jnp.int32, (HEAD_DIM, width), 1) + place
    )
    gain_grad = dot(gain_sum, chosen.astype(F32), 1, 0, exact) / math.sqrt(token_count)
    moment_new = beta_one * first_ref[...] + (1.0 - beta_one) * gain_grad
    second_new = beta_two * second_ref[...] + (1.0 - beta_two) * gain_grad * gain_grad
    moment_out[...] = moment_new
    second_out[...] = second_new
    master_out[...] = master_ref[...] - learn_rate * (moment_new / bias_one) / (
        jnp.sqrt(second_new / bias_two) + adam_eps
    )

    loop(heads - 1, heads, gradients)

    def finish(h):
        for which in range(4):
            save(which, h).wait()

        @pl.when(jnp.logical_not(is_last))
        def _():
            forward_copy(h).wait_send()

        @pl.when(jnp.logical_not(is_first))
        def _():
            backward_copy(h).wait_send()

    loop(0, heads, finish)
    for copy in norm_copies + ctx_copies + dp_copies:
        copy.wait_send()


def body(
    mesh_dims,
    query_rows,
    key_rows,
    value_rows,
    decay_exp,
    out_grad,
    gain_weight,
    master_gain,
    first_moment,
    second_moment,
):
    _, length, row_width = query_rows.shape
    heads = row_width // HEAD_DIM
    n_dp, n_ctx, n_tensor = mesh_dims
    rows = (length, row_width)
    tile = (heads, length, HEAD_DIM)
    state = (heads, HEAD_DIM, HEAD_DIM)
    gain_dims = (heads, HEAD_DIM)
    any_spec = pl.BlockSpec(memory_space=pl.ANY)
    vmem_spec = pl.BlockSpec(memory_space=pltpu.VMEM)
    dma = pltpu.SemaphoreType.DMA
    scratch = (
        [pltpu.VMEM(tile, LOW)] * 4
        + [
            pltpu.VMEM(tile, F32),
            pltpu.VMEM((heads, length, length), F32),
            pltpu.VMEM((heads, length, length), LOW),
            pltpu.VMEM(state, LOW),
        ]
        + [pltpu.VMEM(state, F32)] * 5
        + [pltpu.VMEM(tile, LOW)] * 5
        + [
            pltpu.VMEM(gain_dims, F32),
            pltpu.VMEM(gain_dims, F32),
            pltpu.VMEM((length, HEAD_DIM), F32),
            pltpu.VMEM((length, HEAD_DIM), F32),
            pltpu.VMEM((8, length), F32),
            pltpu.VMEM((n_tensor - 1, 8, length), F32),
            pltpu.VMEM((n_ctx - 1,) + gain_dims, F32),
            pltpu.VMEM(gain_dims, F32),
            pltpu.VMEM((n_dp - 1,) + gain_dims, F32),
            dma((4, heads)),
            dma((4, heads)),
            dma((heads,)),
            dma((heads,)),
            dma((heads,)),
            dma((heads,)),
            dma((n_tensor - 1,)),
            dma((n_tensor - 1,)),
            dma((n_ctx - 1,)),
            dma((n_ctx - 1,)),
            dma((n_dp - 1,)),
            dma((n_dp - 1,)),
        ]
    )
    results = pl.pallas_call(
        functools.partial(fused, (heads, length, n_dp, n_ctx, n_tensor)),
        out_shape=[jax.ShapeDtypeStruct(rows, LOW)] * 4
        + [jax.ShapeDtypeStruct(master_gain.shape, F32)] * 3,
        in_specs=[pl.BlockSpec(memory_space=pltpu.SMEM)] + [any_spec] * 4 + [vmem_spec] * 4,
        out_specs=[any_spec] * 4 + [vmem_spec] * 3,
        scratch_shapes=scratch,
        compiler_params=pltpu.CompilerParams(
            collective_id=0, has_side_effects=True, vmem_limit_bytes=48 * 1024 * 1024
        ),
        name="fused",
    )(
        decay_exp,
        query_rows.reshape(rows),
        key_rows.reshape(rows),
        value_rows.reshape(rows),
        out_grad.reshape(rows),
        gain_weight,
        master_gain,
        first_moment,
        second_moment,
    )
    full = tuple(part.reshape(query_rows.shape) for part in results[:4])
    return full + tuple(results[4:])


def solution(mesh):
    rows = P("dp", "ctx", "tensor")
    share = P("tensor", ("dp", "ctx"))
    mesh_dims = (mesh.shape["dp"], mesh.shape["ctx"], mesh.shape["tensor"])
    return jax.shard_map(
        functools.partial(body, mesh_dims),
        mesh=mesh,
        in_specs=(rows, rows, rows, P("tensor"), rows, P("tensor", None), share, share, share),
        out_specs=(rows, rows, rows, rows, share, share, share),
        check_vma=False,
    )
```

time: 265 us -> 80.5 us (0.30)
  waiting for transfers between devices: 97.7 us -> 0 us
  matrix products: 70.3 us -> 0 us
  Pallas kernels: 0 us -> 67.1 us
  blocking collectives: 26.5 us -> 0 us
  other arithmetic: 24 us -> 0 us
  between operations: 22.4 us -> 0.67 us
  local copies, waits for them, and re-layouts: 22.1 us -> 12.3 us
    all_gather x2 -> x0, waiting for transfers between devices: 85.8 us -> none  [entering(): everything = jax.tree.map(lambda part: lax.all_gather(part, axis), x)]
    dot_general x120 -> x0, matrix products: 70.3 us -> none  [the longest x10 10.3 us: body(): jnp.einsum('bte,bse->bts', grad_blk, value_blk, preferred_element_type=jn...]
    pallas_call x0 -> x1, Pallas kernels: none -> 67.1 us  [body(): pl.pallas_call(functools.partial(fused, (heads, length, n_dp, n_ctx, n_te...]
    select_n x9 -> x0, other arithmetic: 14.2 us -> none  [the longest x8 13.8 us: hop(): return jax.tree.map(lambda a, b: jnp.where(reached, a, b), new, before)]
    unnamed x1 -> x0, blocking collectives: 13.6 us -> none
    psum x2 -> x0, blocking collectives: 12.9 us -> none  [the longest x1 6.49 us: body(): dot_sum = lax.psum(jnp.sum(scaled_grad * attn_all, axis=2), 'tensor')]
    unnamed x6 -> x0, waiting for transfers between devices: 11.9 us -> none
    mul x8 -> x0, local copies, waits for them, and re-layouts: 5.45 us -> none  [combine_states(): later[1][None, :, None, None] * earlier[0] + later[0]]
  transfers between devices with their start and end apart: 4 -> 0, of which waited for: 4 -> 0; matrix products, arithmetic and copies ran while one was open for 11% -> 0% of each run, Pallas kernels for 0% -> 0%
where the time goes in v1:
time: 80.5 us; the launch traced here: 80.1 us
  Pallas kernels  67.1 us (83%)
  local copies, waits for them, and re-layouts  12.3 us (15%)
    pallas_call x1, Pallas kernels, body(): pl.pallas_call(functools.partial(fused, (heads, length, n_dp, n_ctx, n_te...  67.1 us
    unnamed x25, local copies, waits for them, and re-layouts  12.3 us

profile of v1, /device:TPU:0, one launch (start us, length us, event | category | flops | bytes accessed | tf_op | source)
XLA Modules:
  0.0 80.1 jit_solution(8443519771615180087)
XLA Ops:
  0.6 0.0 copy-start.7
  0.6 0.0 copy-start.8
  0.7 0.7 copy-done.7
  1.3 0.0 copy-done.8
  1.3 0.0 copy-start
  1.3 1.1 %copy-done = bf16[1,256,1280]{2,1,0:T(8,128)(2,1)S(1)} copy-done((bf16[1,256,1280]{2,1,0:T(8,128)(2,1)S(1)}, bf16[1,256,1280]{2,1,0:T(8,128)(2,1)}, u32[]{:S(2)}) %copy-start) | copy-done | bytes 655384
  2.4 0.0 copy-start.1
  2.4 1.1 %copy-done.1 = bf16[1,256,1280]{2,1,0:T(8,128)(2,1)S(1)} copy-done((bf16[1,256,1280]{2,1,0:T(8,128)(2,1)S(1)}, bf16[1,256,1280]{2,1,0:T(8,128)(2,1)}, u32[]{:S(2)}) %copy-start.1) | copy-done | bytes 655384
  3.5 0.0 copy-start.2
  3.5 1.1 %copy-done.2 = bf16[1,256,1280]{2,1,0:T(8,128)(2,1)S(1)} copy-done((bf16[1,256,1280]{2,1,0:T(8,128)(2,1)S(1)}, bf16[1,256,1280]{2,1,0:T(8,128)(2,1)}, u32[]{:S(2)}) %copy-start.2) | copy-done | bytes 655384
  4.6 0.0 copy-start.3
  4.6 1.1 %copy-done.3 = bf16[1,256,1280]{2,1,0:T(8,128)(2,1)S(1)} copy-done((bf16[1,256,1280]{2,1,0:T(8,128)(2,1)S(1)}, bf16[1,256,1280]{2,1,0:T(8,128)(2,1)}, u32[]{:S(2)}) %copy-start.3) | copy-done | bytes 655384
  5.7 0.0 copy-start.4
  5.7 0.7 copy-done.4
  6.4 0.0 copy-start.5
  6.4 0.7 copy-done.5
  7.1 0.0 copy-start.6
  7.1 0.7 copy-done.6
  7.8 67.1 %fused.1 = (bf16[256,1280]{1,0:T(8,128)(2,1)S(1)}, bf16[256,1280]{1,0:T(8,128)(2,1)S(1)}, bf16[256,1280]{1,0:T(8,128)(2,1)S(1)}, bf16[256,1280]{1,0:T(8,128)(2,1...) custom-call(s32[10]{0:T(128)S(1)} %copy-done.8, bf16[256,1280]{1,0:T(8,128)(2,1)S(1)} %bitcast.12, ...), custom_call_target="tpu_custom_call" | custom-call | tf_op jit(solution)/shard_map/fused/pallas_call | solution.py:427
  74.9 0.8 %copy.23 = bf16[1,256,1280]{2,1,0:T(8,128)(2,1)} copy(bf16[1,256,1280]{2,1,0:T(8,128)(2,1)S(1)} %bitcast.11) | data formatting | bytes 1310720
  75.8 0.8 %copy.24 = bf16[1,256,1280]{2,1,0:T(8,128)(2,1)} copy(bf16[1,256,1280]{2,1,0:T(8,128)(2,1)S(1)} %bitcast.10) | data formatting | bytes 1310720
  76.6 0.8 %copy.25 = bf16[1,256,1280]{2,1,0:T(8,128)(2,1)} copy(bf16[1,256,1280]{2,1,0:T(8,128)(2,1)S(1)} %bitcast.9) | data formatting | bytes 1310720
  77.4 0.8 %copy.26 = bf16[1,256,1280]{2,1,0:T(8,128)(2,1)} copy(bf16[1,256,1280]{2,1,0:T(8,128)(2,1)S(1)} %bitcast.8) | data formatting | bytes 1310720
  78.3 0.6 copy.27
  78.9 0.6 copy.28
  79.5 0.6 copy.29
Async XLA Ops:
  0.6 0.7 copy-start.7
  0.6 0.7 copy-start.8
  1.3 1.1 %copy-start = (bf16[1,256,1280]{2,1,0:T(8,128)(2,1)S(1)}, bf16[1,256,1280]{2,1,0:T(8,128)(2,1)}, u32[]{:S(2)}) copy-start(bf16[1,256,1280]{2,1,0:T(8,128)(2,1)} %param.9) | copy-start | bytes 1966084
  2.4 1.1 %copy-start.1 = (bf16[1,256,1280]{2,1,0:T(8,128)(2,1)S(1)}, bf16[1,256,1280]{2,1,0:T(8,128)(2,1)}, u32[]{:S(2)}) copy-start(bf16[1,256,1280]{2,1,0:T(8,128)(2,1)} %param.10) | copy-start | bytes 1966084
  3.5 1.1 %copy-start.2 = (bf16[1,256,1280]{2,1,0:T(8,128)(2,1)S(1)}, bf16[1,256,1280]{2,1,0:T(8,128)(2,1)}, u32[]{:S(2)}) copy-start(bf16[1,256,1280]{2,1,0:T(8,128)(2,1)} %param.11) | copy-start | bytes 1966084
  4.6 1.1 %copy-start.3 = (bf16[1,256,1280]{2,1,0:T(8,128)(2,1)S(1)}, bf16[1,256,1280]{2,1,0:T(8,128)(2,1)}, u32[]{:S(2)}) copy-start(bf16[1,256,1280]{2,1,0:T(8,128)(2,1)} %param.13) | copy-start | bytes 1966084
  5.7 0.7 copy-start.4
  6.4 0.7 copy-start.5
  7.1 0.7 copy-start.6

commit v2 on v1

--- a/solution.py
+++ b/solution.py
@@ -31,26 +31,31 @@
 
 def fused(
     dims,
-    exp_ref,
+    exp_hbm,
     query_hbm,
     key_hbm,
     value_hbm,
     grad_hbm,
+    gain_hbm,
+    master_hbm,
+    first_hbm,
+    second_hbm,
+    attn_out,
+    qgrad_out,
+    kgrad_out,
+    vgrad_out,
+    master_out,
+    moment_out,
+    second_out,
+    exp_ref,
+    query_v,
+    key_v,
+    value_v,
+    grad_v,
     gain_ref,
     master_ref,
     first_ref,
     second_ref,
-    attn_hbm,
-    qgrad_hbm,
-    kgrad_hbm,
-    vgrad_hbm,
-    master_out,
-    moment_out,
-    second_out,
-    query_v,
-    key_v,
-    value_v,
-    grad_v,
     attn_v,
     mask_v,
     weight_v,
@@ -61,10 +66,6 @@
     bwd_in,
     bwd_out,
     gl_v,
-    ao_v,
-    qg_v,
-    kg_v,
-    vg_v,
     gain_v,
     gpart_v,
     square_acc,
@@ -75,7 +76,6 @@
     dp_mine,
     dp_in,
     in_sem,
-    out_sem,
     fs_sem,
     fr_sem,
     bs_sem,
@@ -99,31 +99,25 @@
     def columns(h):
         return pl.ds(pl.multiple_of(h * HEAD_DIM, HEAD_DIM), HEAD_DIM)
 
-    pairs = ((key_hbm, key_v), (value_hbm, value_v), (query_hbm, query_v), (grad_hbm, grad_v))
-
-    def load(which, h):
-        hbm, vmem = pairs[which]
-        return pltpu.make_async_copy(hbm.at[:, columns(h)], vmem.at[h], in_sem.at[which, h])
-
-    outs = ((ao_v, attn_hbm), (qg_v, qgrad_hbm), (kg_v, kgrad_hbm), (vg_v, vgrad_hbm))
-
-    def save(which, h):
-        vmem, hbm = outs[which]
-        return pltpu.make_async_copy(vmem.at[h], hbm.at[:, columns(h)], out_sem.at[which, h])
+    pairs = (
+        (exp_hbm, exp_ref),
+        (key_hbm, key_v),
+        (value_hbm, value_v),
+        (query_hbm, query_v),
+        (grad_hbm, grad_v),
+        (gain_hbm, gain_ref),
+        (master_hbm, master_ref),
+        (first_hbm, first_ref),
+        (second_hbm, second_ref),
+    )
+    loads = [
+        pltpu.make_async_copy(hbm, local, in_sem.at[i]) for i, (hbm, local) in enumerate(pairs)
+    ]
+    for copy in loads:
+        copy.start()
 
     def loop(low, high, step):
         lax.fori_loop(low, high, lambda h, c: (step(h), c)[1], 0)
-
-    def start_kv(h):
-        load(0, h).start()
-        load(1, h).start()
-
-    def start_qg(h):
-        load(2, h).start()
-        load(3, h).start()
-
-    loop(0, heads, start_kv)
-    loop(0, heads, start_qg)
 
     barrier = pltpu.get_barrier_semaphore()
     groups = (("dp", at_dp, n_dp), ("ctx", at_ctx, n_ctx), ("tensor", at_tensor, n_tensor))
@@ -167,7 +161,6 @@
             device_id_type=MESH,
         )
 
-    gain_v[...] = gain_ref[...].astype(F32)
     row = lax.broadcasted_iota(jnp.int32, (length, HEAD_DIM), 0).astype(F32)
 
     def rate_of(h):
@@ -183,10 +176,8 @@
         return jnp.exp(jnp.full((HEAD_DIM, HEAD_DIM), -rate_of(h) * length, F32))
 
     def summarize(h):
-        load(0, h).wait()
-        load(1, h).wait()
-        scaled = (key_decay(h) * key_v[h].astype(F32)).astype(LOW)
-        summary = dot(scaled, value_v[h], 0, 0)
+        scaled = (key_decay(h) * key_v[:, columns(h)].astype(F32)).astype(LOW)
+        summary = dot(scaled, value_v[:, columns(h)], 0, 0)
 
         @pl.when(is_first)
         def _():
@@ -197,23 +188,26 @@
         def _():
             local_v[h] = summary
 
+    for copy in loads[:3]:
+        copy.wait()
     loop(0, heads, summarize)
+    for copy in loads[3:]:
+        copy.wait()
+    gain_v[...] = gain_ref[...].astype(F32)
     square_acc[...] = jnp.zeros_like(square_acc)
     dot_acc[...] = jnp.zeros_like(dot_acc)
 
     def attend(h):
-        load(2, h).wait()
-        load(3, h).wait()
         gap = (
             lax.broadcasted_iota(jnp.int32, (length, length), 0)
             - lax.broadcasted_iota(jnp.int32, (length, length), 1)
         ).astype(F32)
         mask = jnp.where(gap >= 0, jnp.exp(-rate_of(h) * jnp.maximum(gap, 0.0)), 0.0)
         mask_v[h] = mask
-        query = query_v[h]
-        weights = (dot(query, key_v[h], 1, 1) * mask).astype(LOW)
+        query = query_v[:, columns(h)]
+        weights = (dot(query, key_v[:, columns(h)], 1, 1) * mask).astype(LOW)
         weight_v[h] = weights
-        attn_v[h] = dot(weights, value_v[h], 1, 0)
+        attn_v[h] = dot(weights, value_v[:, columns(h)], 1, 0)
 
         @pl.when(is_first)
         def _():
@@ -230,10 +224,10 @@
 
             low_v[h] = fwd_in[h].astype(LOW)
 
-        attn = attn_v[h] + query_decay(h) * dot(query_v[h], low_v[h], 1, 0)
+        attn = attn_v[h] + query_decay(h) * dot(query_v[:, columns(h)], low_v[h], 1, 0)
         attn_v[h] = attn
         square_acc[...] += attn * attn
-        dot_acc[...] += grad_v[h].astype(F32) * gain_v[pl.ds(h, 1), :] * attn
+        dot_acc[...] += grad_v[:, columns(h)].astype(F32) * gain_v[pl.ds(h, 1), :] * attn
 
     loop(0, heads, attend)
 
@@ -262,10 +256,10 @@
         attn = attn_v[h]
         inverse = square_acc[...]
         gain = gain_v[pl.ds(h, 1), :]
-        grad = grad_v[h].astype(F32)
+        grad = grad_v[:, columns(h)].astype(F32)
         grad_low = (inverse * (grad * gain - attn * dot_acc[...])).astype(LOW)
         gl_v[h] = grad_low
-        scaled = (query_decay(h) * query_v[h].astype(F32)).astype(LOW)
+        scaled = (query_decay(h) * query_v[:, columns(h)].astype(F32)).astype(LOW)
         part = dot(scaled, grad_low, 0, 0)
 
         @pl.when(is_last)
@@ -278,8 +272,7 @@
             local_v[h] = part
 
         normed = attn * inverse
-        ao_v[h] = (gain * normed).astype(LOW)
-        save(0, h).start()
+        attn_out[:, columns(h)] = (gain * normed).astype(LOW)
         gpart_v[pl.ds(h, 1), :] = jnp.sum(grad * normed, axis=0, keepdims=True)
 
     loop(0, heads, back_summary)
@@ -289,18 +282,17 @@
 
     def gradients(h):
         grad_low = gl_v[h]
-        dweights = (dot(grad_low, value_v[h], 1, 1) * mask_v[h]).astype(LOW)
-        query_part = dot(dweights, key_v[h], 1, 0)
+        dweights = (dot(grad_low, value_v[:, columns(h)], 1, 1) * mask_v[h]).astype(LOW)
+        query_part = dot(dweights, key_v[:, columns(h)], 1, 0)
         query_part += query_decay(h) * dot(grad_low, low_v[h], 1, 1)
-        qg_v[h] = query_part.astype(LOW)
-        save(1, h).start()
-        key_part = dot(dweights, query_v[h], 0, 0)
+        qgrad_out[:, columns(h)] = query_part.astype(LOW)
+        key_part = dot(dweights, query_v[:, columns(h)], 0, 0)
         value_part = dot(weight_v[h], grad_low, 0, 0)
 
         @pl.when(is_last)
         def _():
-            kg_v[h] = key_part.astype(LOW)
-            vg_v[h] = value_part.astype(LOW)
+            kgrad_out[:, columns(h)] = key_part.astype(LOW)
+            vgrad_out[:, columns(h)] = value_part.astype(LOW)
 
         @pl.when(jnp.logical_not(is_last))
         def _():
@@ -313,11 +305,9 @@
 
             back_low = bwd_in[h].astype(LOW)
             decay = key_decay(h)
-            kg_v[h] = (key_part + decay * dot(value_v[h], back_low, 1, 1)).astype(LOW)
-            vg_v[h] = (value_part + decay * dot(key_v[h], back_low, 1, 0)).astype(LOW)
-
-        save(2, h).start()
-        save(3, h).start()
+            kgrad_out[:, columns(h)] = (key_part + decay * dot(value_v[:, columns(h)], back_low, 1, 1)).astype(LOW)
+            vgrad_out[:, columns(h)] = (value_part + decay * dot(key_v[:, columns(h)], back_low, 1, 0)).astype(LOW)
+
 
     third = heads // 3
     loop(0, third, gradients)
@@ -352,9 +342,6 @@
     loop(heads - 1, heads, gradients)
 
     def finish(h):
-        for which in range(4):
-            save(which, h).wait()
-
         @pl.when(jnp.logical_not(is_last))
         def _():
             forward_copy(h).wait_send()
@@ -366,6 +353,18 @@
     loop(0, heads, finish)
     for copy in norm_copies + ctx_copies + dp_copies:
         copy.wait_send()
+
+
+def store_all(*refs):
+    sems = refs[14]
+    copies = [
+        pltpu.make_async_copy(source, target, sems.at[i])
+        for i, (source, target) in enumerate(zip(refs[:7], refs[7:14]))
+    ]
+    for copy in copies:
+        copy.start()
+    for copy in copies:
+        copy.wait()
 
 
 def body(
@@ -387,11 +386,14 @@
     tile = (heads, length, HEAD_DIM)
     state = (heads, HEAD_DIM, HEAD_DIM)
     gain_dims = (heads, HEAD_DIM)
-    any_spec = pl.BlockSpec(memory_space=pl.ANY)
+    hbm_spec = pl.BlockSpec(memory_space=pltpu.HBM)
     vmem_spec = pl.BlockSpec(memory_space=pltpu.VMEM)
     dma = pltpu.SemaphoreType.DMA
     scratch = (
-        [pltpu.VMEM(tile, LOW)] * 4
+        [pltpu.SMEM((heads,), jnp.int32)]
+        + [pltpu.VMEM(rows, LOW)] * 4
+        + [pltpu.VMEM(gain_dims, LOW)]
+        + [pltpu.VMEM(master_gain.shape, F32)] * 3
         + [
             pltpu.VMEM(tile, F32),
             pltpu.VMEM((heads, length, length), F32),
@@ -399,8 +401,8 @@
             pltpu.VMEM(state, LOW),
         ]
         + [pltpu.VMEM(state, F32)] * 5
-        + [pltpu.VMEM(tile, LOW)] * 5
         + [
+            pltpu.VMEM(tile, LOW),
             pltpu.VMEM(gain_dims, F32),
             pltpu.VMEM(gain_dims, F32),
             pltpu.VMEM((length, HEAD_DIM), F32),
@@ -410,29 +412,22 @@
             pltpu.VMEM((n_ctx - 1,) + gain_dims, F32),
             pltpu.VMEM(gain_dims, F32),
             pltpu.VMEM((n_dp - 1,) + gain_dims, F32),
-            dma((4, heads)),
-            dma((4, heads)),
-            dma((heads,)),
-            dma((heads,)),
-            dma((heads,)),
-            dma((heads,)),
-            dma((n_tensor - 1,)),
-            dma((n_tensor - 1,)),
-            dma((n_ctx - 1,)),
-            dma((n_ctx - 1,)),
-            dma((n_dp - 1,)),
-            dma((n_dp - 1,)),
+            dma((9,)),
         ]
-    )
-    results = pl.pallas_call(
+        + [dma((heads,))] * 4
+        + [dma((count - 1,)) for count in (n_tensor, n_tensor, n_ctx, n_ctx, n_dp, n_dp)]
+    )
+    out_shape = [jax.ShapeDtypeStruct(rows, LOW)] * 4 + [
+        jax.ShapeDtypeStruct(master_gain.shape, F32)
+    ] * 3
+    held = pl.pallas_call(
         functools.partial(fused, (heads, length, n_dp, n_ctx, n_tensor)),
-        out_shape=[jax.ShapeDtypeStruct(rows, LOW)] * 4
-        + [jax.ShapeDtypeStruct(master_gain.shape, F32)] * 3,
-        in_specs=[pl.BlockSpec(memory_space=pltpu.SMEM)] + [any_spec] * 4 + [vmem_spec] * 4,
-        out_specs=[any_spec] * 4 + [vmem_spec] * 3,
+        out_shape=out_shape,
+        in_specs=[hbm_spec] * 9,
+        out_specs=[vmem_spec] * 7,
         scratch_shapes=scratch,
         compiler_params=pltpu.CompilerParams(
-            collective_id=0, has_side_effects=True, vmem_limit_bytes=48 * 1024 * 1024
+            collective_id=0, has_side_effects=True, vmem_limit_bytes=67043328
         ),
         name="fused",
     )(
@@ -446,6 +441,14 @@
         first_moment,
         second_moment,
     )
+    results = pl.pallas_call(
+        store_all,
+        out_shape=out_shape,
+        in_specs=[vmem_spec] * 7,
+        out_specs=[hbm_spec] * 7,
+        scratch_shapes=[dma((7,))],
+        name="store_all",
+    )(*held)
     full = tuple(part.reshape(query_rows.shape) for part in results[:4])
     return full + tuple(results[4:])
 

time: 80.5 us -> 70.5 us (0.88)
  local copies, waits for them, and re-layouts: 12.3 us -> 0 us
  Pallas kernels: 67.1 us -> 69.7 us
    unnamed x25 -> x0, local copies, waits for them, and re-layouts: 12.3 us -> none
    pallas_call x0 -> x1, Pallas kernels: none -> 3.25 us  [body(): pl.pallas_call(store_all, out_shape=out_shape, in_specs=[vmem_spec] * 7,...]
where the time goes in v2:
time: 70.5 us; the launch traced here: 70.3 us
  Pallas kernels  69.7 us (99%)
    pallas_call x1, Pallas kernels, body(): pl.pallas_call(functools.partial(fused, (heads, length, n_dp, n_ctx, n_te...  66.4 us
    pallas_call x1, Pallas kernels, body(): pl.pallas_call(store_all, out_shape=out_shape, in_specs=[vmem_spec] * 7,...  3.25 us

profile of v2, /device:TPU:0, one launch (start us, length us, event | category | flops | bytes accessed | tf_op | source)
XLA Modules:
  0.0 70.3 jit_solution(17036078039800932367)
XLA Ops:
  0.6 66.4 %fused.1 = (bf16[256,1280]{1,0:T(8,128)(2,1)}, bf16[256,1280]{1,0:T(8,128)(2,1)}, bf16[256,1280]{1,0:T(8,128)(2,1)}, bf16[256,1280]{1,0:T(8,128)(2,1)}, f32[10,1...) custom-call(s32[10]{0:T(128)} %exp_hbm.1, bf16[256,1280]{1,0:T(8,128)(2,1)} %bitcast.8, bf16[256,1280]{1,0:T(8,128)(2,1)} %bitcast.9, ...), custom_call_target="tpu_custom_call" | custom-call | tf_op jit(solution)/shard_map/fused/pallas_call | solution.py:423
  67.1 3.3 %store_all.1 = (bf16[256,1280]{1,0:T(8,128)(2,1)}, bf16[256,1280]{1,0:T(8,128)(2,1)}, bf16[256,1280]{1,0:T(8,128)(2,1)}, bf16[256,1280]{1,0:T(8,128)(2,1)}, f32[...) custom-call(bf16[256,1280]{1,0:T(8,128)(2,1)} %get-tuple-element.21.refs_0_, ...), custom_call_target="tpu_custom_call" | custom-call | tf_op jit(solution)/shard_map/store_all/pallas_call | solution.py:444

commit v3 on v2

--- a/solution.py
+++ b/solution.py
@@ -9,6 +9,7 @@
 from jax.sharding import PartitionSpec as P
 
 HEAD_DIM = 128
+PARTS = 2
 MESH = pl.DeviceIdType.MESH
 
 beta_one = 0.9
@@ -40,13 +41,17 @@
     master_hbm,
     first_hbm,
     second_hbm,
+    attn_hbm,
+    qgrad_hbm,
+    kgrad_hbm,
+    vgrad_hbm,
+    master_out,
+    moment_out,
+    second_out,
     attn_out,
     qgrad_out,
     kgrad_out,
     vgrad_out,
-    master_out,
-    moment_out,
-    second_out,
     exp_ref,
     query_v,
     key_v,
@@ -76,6 +81,8 @@
     dp_mine,
     dp_in,
     in_sem,
+    attn_sem,
+    out_sem,
     fs_sem,
     fr_sem,
     bs_sem,
@@ -113,11 +120,17 @@
     loads = [
         pltpu.make_async_copy(hbm, local, in_sem.at[i]) for i, (hbm, local) in enumerate(pairs)
     ]
-    for copy in loads:
-        copy.start()
-
     def loop(low, high, step):
         lax.fori_loop(low, high, lambda h, c: (step(h), c)[1], 0)
+
+    attn_save = pltpu.make_async_copy(attn_out, attn_hbm, attn_sem.at[0])
+    outs = ((qgrad_out, qgrad_hbm), (kgrad_out, kgrad_hbm), (vgrad_out, vgrad_hbm))
+
+    def save(which, h):
+        local, hbm = outs[which]
+        return pltpu.make_async_copy(
+            local.at[:, columns(h)], hbm.at[:, columns(h)], out_sem.at[which, h]
+        )
 
     barrier = pltpu.get_barrier_semaphore()
     groups = (("dp", at_dp, n_dp), ("ctx", at_ctx, n_ctx), ("tensor", at_tensor, n_tensor))
@@ -126,7 +139,8 @@
             pl.semaphore_signal(
                 barrier, inc=1, device_id={name: lax.rem(mine + d, count)}, device_id_type=MESH
             )
-    pl.semaphore_wait(barrier, n_dp + n_ctx + n_tensor - 3)
+    for copy in loads:
+        copy.start()
 
     def share(name, mine, count, source, slots, send_sem, recv_sem):
         return [
@@ -141,22 +155,27 @@
             for d in range(1, count)
         ]
 
-    def forward_copy(h):
+    part_rows = HEAD_DIM // PARTS
+
+    def some_rows(part):
+        return pl.ds(part * part_rows, part_rows)
+
+    def forward_copy(h, part):
         return pltpu.make_async_remote_copy(
-            src_ref=fwd_out.at[h],
-            dst_ref=fwd_in.at[h],
-            send_sem=fs_sem.at[h],
-            recv_sem=fr_sem.at[h],
+            src_ref=fwd_out.at[h, some_rows(part)],
+            dst_ref=fwd_in.at[h, some_rows(part)],
+            send_sem=fs_sem.at[h, part],
+            recv_sem=fr_sem.at[h, part],
             device_id={"ctx": later},
             device_id_type=MESH,
         )
 
-    def backward_copy(h):
+    def backward_copy(h, part):
         return pltpu.make_async_remote_copy(
-            src_ref=bwd_out.at[h],
-            dst_ref=bwd_in.at[h],
-            send_sem=bs_sem.at[h],
-            recv_sem=br_sem.at[h],
+            src_ref=bwd_out.at[h, some_rows(part)],
+            dst_ref=bwd_in.at[h, some_rows(part)],
+            send_sem=bs_sem.at[h, part],
+            recv_sem=br_sem.at[h, part],
             device_id={"ctx": earlier},
             device_id_type=MESH,
         )
@@ -173,7 +192,7 @@
         return jnp.exp(-rate_of(h) * row)
 
     def block_decay(h):
-        return jnp.exp(jnp.full((HEAD_DIM, HEAD_DIM), -rate_of(h) * length, F32))
+        return jnp.exp(jnp.full((part_rows, HEAD_DIM), -rate_of(h) * length, F32))
 
     def summarize(h):
         scaled = (key_decay(h) * key_v[:, columns(h)].astype(F32)).astype(LOW)
@@ -182,7 +201,6 @@
         @pl.when(is_first)
         def _():
             fwd_out[h] = summary
-            forward_copy(h).start()
 
         @pl.when(jnp.logical_not(is_first))
         def _():
@@ -191,6 +209,16 @@
     for copy in loads[:3]:
         copy.wait()
     loop(0, heads, summarize)
+    pl.semaphore_wait(barrier, n_dp + n_ctx + n_tensor - 3)
+
+    @pl.when(is_first)
+    def _():
+        def send(h):
+            for part in range(PARTS):
+                forward_copy(h, part).start()
+
+        loop(0, heads, send)
+
     for copy in loads[3:]:
         copy.wait()
     gain_v[...] = gain_ref[...].astype(F32)
@@ -215,12 +243,14 @@
 
         @pl.when(jnp.logical_not(is_first))
         def _():
-            forward_copy(h).wait_recv()
-
-            @pl.when(jnp.logical_not(is_last))
-            def _():
-                fwd_out[h] = block_decay(h) * fwd_in[h] + local_v[h]
-                forward_copy(h).start()
+            for part in range(PARTS):
+                rows = some_rows(part)
+                forward_copy(h, part).wait_recv()
+
+                @pl.when(jnp.logical_not(is_last))
+                def _():
+                    fwd_out[h, rows] = block_decay(h) * fwd_in[h, rows] + local_v[h, rows]
+                    forward_copy(h, part).start()
 
             low_v[h] = fwd_in[h].astype(LOW)
 
@@ -265,7 +295,8 @@
         @pl.when(is_last)
         def _():
             bwd_out[h] = part
-            backward_copy(h).start()
+            for piece in range(PARTS):
+                backward_copy(h, piece).start()
 
         @pl.when(jnp.logical_not(is_last))
         def _():
@@ -276,6 +307,7 @@
         gpart_v[pl.ds(h, 1), :] = jnp.sum(grad * normed, axis=0, keepdims=True)
 
     loop(0, heads, back_summary)
+    attn_save.start()
     ctx_copies = share("ctx", at_ctx, n_ctx, gpart_v, ctx_in, cs_sem, cr_sem)
     for copy in ctx_copies:
         copy.start()
@@ -296,21 +328,25 @@
 
         @pl.when(jnp.logical_not(is_last))
         def _():
-            backward_copy(h).wait_recv()
-
-            @pl.when(jnp.logical_not(is_first))
-            def _():
-                bwd_out[h] = block_decay(h) * bwd_in[h] + local_v[h]
-                backward_copy(h).start()
+            for part in range(PARTS):
+                rows = some_rows(part)
+                backward_copy(h, part).wait_recv()
+
+                @pl.when(jnp.logical_not(is_first))
+                def _():
+                    bwd_out[h, rows] = block_decay(h) * bwd_in[h, rows] + local_v[h, rows]
+                    backward_copy(h, part).start()
 
             back_low = bwd_in[h].astype(LOW)
             decay = key_decay(h)
             kgrad_out[:, columns(h)] = (key_part + decay * dot(value_v[:, columns(h)], back_low, 1, 1)).astype(LOW)
             vgrad_out[:, columns(h)] = (value_part + decay * dot(key_v[:, columns(h)], back_low, 1, 0)).astype(LOW)
 
-
-    third = heads // 3
-    loop(0, third, gradients)
+        for which in range(3):
+            save(which, h).start()
+
+
+    loop(0, heads - 2, gradients)
     gain_sum = gpart_v[...]
     for d, copy in enumerate(ctx_copies):
         copy.wait_recv()
@@ -319,7 +355,7 @@
     dp_copies = share("dp", at_dp, n_dp, dp_mine, dp_in, ds_sem, dr_sem)
     for copy in dp_copies:
         copy.start()
-    loop(third, heads - 1, gradients)
+    loop(heads - 2, heads, gradients)
 
     gain_sum = dp_mine[...]
     for d, copy in enumerate(dp_copies):
@@ -339,16 +375,21 @@
         jnp.sqrt(second_new / bias_two) + adam_eps
     )
 
-    loop(heads - 1, heads, gradients)
+    attn_save.wait()
 
     def finish(h):
+        for which in range(3):
+            save(which, h).wait()
+
         @pl.when(jnp.logical_not(is_last))
         def _():
-            forward_copy(h).wait_send()
+            for part in range(PARTS):
+                forward_copy(h, part).wait_send()
 
         @pl.when(jnp.logical_not(is_first))
         def _():
-            backward_copy(h).wait_send()
+            for part in range(PARTS):
+                backward_copy(h, part).wait_send()
 
     loop(0, heads, finish)
     for copy in norm_copies + ctx_copies + dp_copies:
@@ -356,14 +397,23 @@
 
 
 def store_all(*refs):
-    sems = refs[14]
-    copies = [
-        pltpu.make_async_copy(source, target, sems.at[i])
-        for i, (source, target) in enumerate(zip(refs[:7], refs[7:14]))
+    count = len(refs) // 3
+    sources, targets, held = refs[:count], refs[count : 2 * count], refs[2 * count : 3 * count]
+    sems = refs[3 * count]
+    reads = [
+        pltpu.make_async_copy(source, local, sems.at[0, i])
+        for i, (source, local) in enumerate(zip(sources, held))
     ]
-    for copy in copies:
+    writes = [
+        pltpu.make_async_copy(local, target, sems.at[1, i])
+        for i, (target, local) in enumerate(zip(targets, held))
+    ]
+    for copy in reads:
         copy.start()
-    for copy in copies:
+    for read, write in zip(reads, writes):
+        read.wait()
+        write.start()
+    for copy in writes:
         copy.wait()
 
 
@@ -390,7 +440,8 @@
     vmem_spec = pl.BlockSpec(memory_space=pltpu.VMEM)
     dma = pltpu.SemaphoreType.DMA
     scratch = (
-        [pltpu.SMEM((heads,), jnp.int32)]
+        [pltpu.VMEM(rows, LOW)] * 4
+        + [pltpu.SMEM((heads,), jnp.int32)]
         + [pltpu.VMEM(rows, LOW)] * 4
         + [pltpu.VMEM(gain_dims, LOW)]
         + [pltpu.VMEM(master_gain.shape, F32)] * 3
@@ -413,8 +464,10 @@
             pltpu.VMEM(gain_dims, F32),
             pltpu.VMEM((n_dp - 1,) + gain_dims, F32),
             dma((9,)),
+            dma((1,)),
+            dma((3, heads)),
         ]
-        + [dma((heads,))] * 4
+        + [dma((heads, PARTS))] * 4
         + [dma((count - 1,)) for count in (n_tensor, n_tensor, n_ctx, n_ctx, n_dp, n_dp)]
     )
     out_shape = [jax.ShapeDtypeStruct(rows, LOW)] * 4 + [
@@ -424,7 +477,7 @@
         functools.partial(fused, (heads, length, n_dp, n_ctx, n_tensor)),
         out_shape=out_shape,
         in_specs=[hbm_spec] * 9,
-        out_specs=[vmem_spec] * 7,
+        out_specs=[hbm_spec] * 4 + [vmem_spec] * 3,
         scratch_shapes=scratch,
         compiler_params=pltpu.CompilerParams(
             collective_id=0, has_side_effects=True, vmem_limit_bytes=67043328
@@ -444,9 +497,10 @@
     results = pl.pallas_call(
         store_all,
         out_shape=out_shape,
-        in_specs=[vmem_spec] * 7,
+        in_specs=[hbm_spec] * 7,
         out_specs=[hbm_spec] * 7,
-        scratch_shapes=[dma((7,))],
+        scratch_shapes=[pltpu.VMEM(part.shape, part.dtype) for part in out_shape] + [dma((2, 7))],
+        compiler_params=pltpu.CompilerParams(vmem_limit_bytes=67043328),
         name="store_all",
     )(*held)
     full = tuple(part.reshape(query_rows.shape) for part in results[:4])

time: 70.5 us -> 62 us (0.88)
  Pallas kernels: 69.7 us -> 61.2 us
    pallas_call x1, Pallas kernels: 66.4 us -> 58.5 us  [body(): pl.pallas_call(functools.partial(fused, (heads, length, n_dp, n_ctx, n_te...]
where the time goes in v3:
time: 62 us; the launch traced here: 61.8 us
  Pallas kernels  61.2 us (99%)
  between operations  0.64 us (1%)
    pallas_call x1, Pallas kernels, body(): pl.pallas_call(functools.partial(fused, (heads, length, n_dp, n_ctx, n_te...  58.5 us
    pallas_call x1, Pallas kernels, body(): pl.pallas_call(store_all, out_shape=out_shape, in_specs=[hbm_spec] * 7, o...  2.7 us

profile of v3, /device:TPU:0, one launch (start us, length us, event | category | flops | bytes accessed | tf_op | source)
XLA Modules:
  0.0 61.8 jit_solution(9772145695579717610)
XLA Ops:
  0.6 58.5 %fused.1 = (bf16[256,1280]{1,0:T(8,128)(2,1)}, bf16[256,1280]{1,0:T(8,128)(2,1)}, bf16[256,1280]{1,0:T(8,128)(2,1)}, bf16[256,1280]{1,0:T(8,128)(2,1)}, f32[10,1...) custom-call(s32[10]{0:T(128)} %exp_hbm.1, bf16[256,1280]{1,0:T(8,128)(2,1)} %bitcast.8, bf16[256,1280]{1,0:T(8,128)(2,1)} %bitcast.9, ...), custom_call_target="tpu_custom_call" | custom-call | tf_op jit(solution)/shard_map/fused/pallas_call | solution.py:476
  59.1 2.7 %store_all.1 = (bf16[256,1280]{1,0:T(8,128)(2,1)}, bf16[256,1280]{1,0:T(8,128)(2,1)}, bf16[256,1280]{1,0:T(8,128)(2,1)}, bf16[256,1280]{1,0:T(8,128)(2,1)}, f32[...) custom-call(bf16[256,1280]{1,0:T(8,128)(2,1)} %get-tuple-element.21.refs_0_, ...), custom_call_target="tpu_custom_call" | custom-call | tf_op jit(solution)/shard_map/store_all/pallas_call | solution.py:497

commit v4 on v3

--- a/solution.py
+++ b/solution.py
@@ -282,6 +282,8 @@
     square_acc[...] = inv_rms
     dot_acc[...] = inv_rms * inv_rms * mean_dot
 
+    early = min(3, heads)
+
     def back_summary(h):
         attn = attn_v[h]
         inverse = square_acc[...]
@@ -295,8 +297,11 @@
         @pl.when(is_last)
         def _():
             bwd_out[h] = part
-            for piece in range(PARTS):
-                backward_copy(h, piece).start()
+
+            @pl.when(h < early)
+            def _():
+                for piece in range(PARTS):
+                    backward_copy(h, piece).start()
 
         @pl.when(jnp.logical_not(is_last))
         def _():
@@ -307,10 +312,20 @@
         gpart_v[pl.ds(h, 1), :] = jnp.sum(grad * normed, axis=0, keepdims=True)
 
     loop(0, heads, back_summary)
-    attn_save.start()
     ctx_copies = share("ctx", at_ctx, n_ctx, gpart_v, ctx_in, cs_sem, cr_sem)
     for copy in ctx_copies:
         copy.start()
+
+    @pl.when(is_last)
+    def _():
+        def send(h):
+            for part in range(PARTS):
+                backward_copy(h, part).start()
+
+        loop(early, heads, send)
+
+
+    attn_save.start()
 
     def gradients(h):
         grad_low = gl_v[h]

time: 62 us -> 60.7 us (0.979)
  Pallas kernels: 61.2 us -> 59.9 us
    pallas_call x1, Pallas kernels: 58.5 us -> 57.2 us  [body(): pl.pallas_call(functools.partial(fused, (heads, length, n_dp, n_ctx, n_te...]
where the time goes in v4:
time: 60.7 us; the launch traced here: 60.5 us
  Pallas kernels  59.9 us (99%)
  between operations  0.64 us (1%)
    pallas_call x1, Pallas kernels, body(): pl.pallas_call(functools.partial(fused, (heads, length, n_dp, n_ctx, n_te...  57.2 us
    pallas_call x1, Pallas kernels, body(): pl.pallas_call(store_all, out_shape=out_shape, in_specs=[hbm_spec] * 7, o...  2.7 us

profile of v4, /device:TPU:0, one launch (start us, length us, event | category | flops | bytes accessed | tf_op | source)
XLA Modules:
  0.0 60.5 jit_solution(2475833486141502999)
XLA Ops:
  0.6 57.2 %fused.1 = (bf16[256,1280]{1,0:T(8,128)(2,1)}, bf16[256,1280]{1,0:T(8,128)(2,1)}, bf16[256,1280]{1,0:T(8,128)(2,1)}, bf16[256,1280]{1,0:T(8,128)(2,1)}, f32[10,1...) custom-call(s32[10]{0:T(128)} %exp_hbm.1, bf16[256,1280]{1,0:T(8,128)(2,1)} %bitcast.8, bf16[256,1280]{1,0:T(8,128)(2,1)} %bitcast.9, ...), custom_call_target="tpu_custom_call" | custom-call | tf_op jit(solution)/shard_map/fused/pallas_call | solution.py:491
  57.8 2.7 %store_all.1 = (bf16[256,1280]{1,0:T(8,128)(2,1)}, bf16[256,1280]{1,0:T(8,128)(2,1)}, bf16[256,1280]{1,0:T(8,128)(2,1)}, bf16[256,1280]{1,0:T(8,128)(2,1)}, f32[...) custom-call(bf16[256,1280]{1,0:T(8,128)(2,1)} %get-tuple-element.21.refs_0_, ...), custom_call_target="tpu_custom_call" | custom-call | tf_op jit(solution)/shard_map/store_all/pallas_call | solution.py:512

commit v5 on v4

--- a/solution.py
+++ b/solution.py
@@ -41,17 +41,13 @@
     master_hbm,
     first_hbm,
     second_hbm,
-    attn_hbm,
-    qgrad_hbm,
-    kgrad_hbm,
-    vgrad_hbm,
-    master_out,
-    moment_out,
-    second_out,
     attn_out,
     qgrad_out,
     kgrad_out,
     vgrad_out,
+    master_out,
+    moment_out,
+    second_out,
     exp_ref,
     query_v,
     key_v,
@@ -81,8 +77,6 @@
     dp_mine,
     dp_in,
     in_sem,
-    attn_sem,
-    out_sem,
     fs_sem,
     fr_sem,
     bs_sem,
@@ -123,15 +117,6 @@
     def loop(low, high, step):
         lax.fori_loop(low, high, lambda h, c: (step(h), c)[1], 0)
 
-    attn_save = pltpu.make_async_copy(attn_out, attn_hbm, attn_sem.at[0])
-    outs = ((qgrad_out, qgrad_hbm), (kgrad_out, kgrad_hbm), (vgrad_out, vgrad_hbm))
-
-    def save(which, h):
-        local, hbm = outs[which]
-        return pltpu.make_async_copy(
-            local.at[:, columns(h)], hbm.at[:, columns(h)], out_sem.at[which, h]
-        )
-
     barrier = pltpu.get_barrier_semaphore()
     groups = (("dp", at_dp, n_dp), ("ctx", at_ctx, n_ctx), ("tensor", at_tensor, n_tensor))
     for name, mine, count in groups:
@@ -325,8 +310,6 @@
         loop(early, heads, send)
 
 
-    attn_save.start()
-
     def gradients(h):
         grad_low = gl_v[h]
         dweights = (dot(grad_low, value_v[:, columns(h)], 1, 1) * mask_v[h]).astype(LOW)
@@ -356,9 +339,6 @@
             decay = key_decay(h)
             kgrad_out[:, columns(h)] = (key_part + decay * dot(value_v[:, columns(h)], back_low, 1, 1)).astype(LOW)
             vgrad_out[:, columns(h)] = (value_part + decay * dot(key_v[:, columns(h)], back_low, 1, 0)).astype(LOW)
-
-        for which in range(3):
-            save(which, h).start()
 
 
     loop(0, heads - 2, gradients)
@@ -390,12 +370,7 @@
         jnp.sqrt(second_new / bias_two) + adam_eps
     )
 
-    attn_save.wait()
-
     def finish(h):
-        for which in range(3):
-            save(which, h).wait()
-
         @pl.when(jnp.logical_not(is_last))
         def _():
             for part in range(PARTS):
@@ -412,23 +387,15 @@
 
 
 def store_all(*refs):
-    count = len(refs) // 3
-    sources, targets, held = refs[:count], refs[count : 2 * count], refs[2 * count : 3 * count]
-    sems = refs[3 * count]
-    reads = [
-        pltpu.make_async_copy(source, local, sems.at[0, i])
-        for i, (source, local) in enumerate(zip(sources, held))
+    count = len(refs) // 2
+    sems = refs[2 * count]
+    copies = [
+        pltpu.make_async_copy(source, target, sems.at[i])
+        for i, (source, target) in enumerate(zip(refs[:count], refs[count : 2 * count]))
     ]
-    writes = [
-        pltpu.make_async_copy(local, target, sems.at[1, i])
-        for i, (target, local) in enumerate(zip(targets, held))
-    ]
-    for copy in reads:
+    for copy in copies:
         copy.start()
-    for read, write in zip(reads, writes):
-        read.wait()
-        write.start()
-    for copy in writes:
+    for copy in copies:
         copy.wait()
 
 
@@ -455,8 +422,7 @@
     vmem_spec = pl.BlockSpec(memory_space=pltpu.VMEM)
     dma = pltpu.SemaphoreType.DMA
     scratch = (
-        [pltpu.VMEM(rows, LOW)] * 4
-        + [pltpu.SMEM((heads,), jnp.int32)]
+        [pltpu.SMEM((heads,), jnp.int32)]
         + [pltpu.VMEM(rows, LOW)] * 4
         + [pltpu.VMEM(gain_dims, LOW)]
         + [pltpu.VMEM(master_gain.shape, F32)] * 3
@@ -479,8 +445,6 @@
             pltpu.VMEM(gain_dims, F32),
             pltpu.VMEM((n_dp - 1,) + gain_dims, F32),
             dma((9,)),
-            dma((1,)),
-            dma((3, heads)),
         ]
         + [dma((heads, PARTS))] * 4
         + [dma((count - 1,)) for count in (n_tensor, n_tensor, n_ctx, n_ctx, n_dp, n_dp)]
@@ -490,12 +454,12 @@
     ] * 3
     held = pl.pallas_call(
         functools.partial(fused, (heads, length, n_dp, n_ctx, n_tensor)),
-        out_shape=out_shape,
+        out_shape=[pltpu.VMEM(part.shape, part.dtype) for part in out_shape],
         in_specs=[hbm_spec] * 9,
-        out_specs=[hbm_spec] * 4 + [vmem_spec] * 3,
+        out_specs=[vmem_spec] * 7,
         scratch_shapes=scratch,
         compiler_params=pltpu.CompilerParams(
-            collective_id=0, has_side_effects=True, vmem_limit_bytes=67043328
+            collective_id=0, has_side_effects=True, vmem_limit_bytes=61*1024*1024
         ),
         name="fused",
     )(
@@ -512,10 +476,10 @@
     results = pl.pallas_call(
         store_all,
         out_shape=out_shape,
-        in_specs=[hbm_spec] * 7,
+        in_specs=[vmem_spec] * 7,
         out_specs=[hbm_spec] * 7,
-        scratch_shapes=[pltpu.VMEM(part.shape, part.dtype) for part in out_shape] + [dma((2, 7))],
-        compiler_params=pltpu.CompilerParams(vmem_limit_bytes=67043328),
+        scratch_shapes=[dma((7,))],
+        compiler_params=pltpu.CompilerParams(vmem_limit_bytes=1024 * 1024),
         name="store_all",
     )(*held)
     full = tuple(part.reshape(query_rows.shape) for part in results[:4])

time: 60.7 us -> 58.6 us (0.965)
  Pallas kernels: 59.9 us -> 57.8 us
    pallas_call x1, Pallas kernels: 2.7 us -> 1.55 us  [body(): pl.pallas_call(store_all, out_shape=out_shape, in_specs=[vmem_spec] * 7,...]
    pallas_call x1, Pallas kernels: 57.2 us -> 56.3 us  [body(): pl.pallas_call(functools.partial(fused, (heads, length, n_dp, n_ctx, n_te...]
where the time goes in v5:
time: 58.6 us; the launch traced here: 58.5 us
  Pallas kernels  57.8 us (99%)
  between operations  0.64 us (1%)
    pallas_call x1, Pallas kernels, body(): pl.pallas_call(functools.partial(fused, (heads, length, n_dp, n_ctx, n_te...  56.3 us
    pallas_call x1, Pallas kernels, body(): pl.pallas_call(store_all, out_shape=out_shape, in_specs=[vmem_spec] * 7,...  1.55 us

profile of v5, /device:TPU:0, one launch (start us, length us, event | category | flops | bytes accessed | tf_op | source)
XLA Modules:
  0.0 58.5 jit_solution(4071107153271020341)
XLA Ops:
  0.6 56.3 %fused.1 = (bf16[256,1280]{1,0:T(8,128)(2,1)S(1)}, bf16[256,1280]{1,0:T(8,128)(2,1)S(1)}, bf16[256,1280]{1,0:T(8,128)(2,1)S(1)}, bf16[256,1280]{1,0:T(8,128)(2,1...) custom-call(s32[10]{0:T(128)} %exp_hbm.1, bf16[256,1280]{1,0:T(8,128)(2,1)} %bitcast.8, ...), custom_call_target="tpu_custom_call" | custom-call | tf_op jit(solution)/shard_map/fused/pallas_call | solution.py:455
  56.9 1.6 %store_all.1 = (bf16[256,1280]{1,0:T(8,128)(2,1)}, bf16[256,1280]{1,0:T(8,128)(2,1)}, bf16[256,1280]{1,0:T(8,128)(2,1)}, bf16[256,1280]{1,0:T(8,128)(2,1)}, f32[...) custom-call(bf16[256,1280]{1,0:T(8,128)(2,1)S(1)} %get-tuple-element.21.refs_0_, ...), custom_call_target="tpu_custom_call" | custom-call | tf_op jit(solution)/shard_map/store_all/pallas_call | solution.py:476
